TPU v7x, 512 devices: a whole 4x4x16 slice. The times are simulated.
512 devices in a mesh: shot: 16 (over z_lo, core), recv: 32 (over z_hi, y, x).
Axes of the slice: x: 4, y: 4, z: 16 (z_hi: 2, z_lo: 8; z = z_hi * 8 + z_lo), core: 2. Of those that a mesh axis runs over, the one named last changes fastest.
Arguments:
- pressure: bfloat16 [2, 6144, 6144], P(None, 'recv', 'shot'), may hold values from -6 to 6
Outputs:
- multiples: float32 [2, 6144, 6144], P(None, 'recv', 'shot')
All inputs are finite; a program needn't handle non-finite values.
Results may differ from a plain program's by a relative error of at most 0.0044.
Values may be sent and summed in bfloat16 or wider, within the bound.
No kernel may reach another device: no remote copies, remote signals or barrier semaphores. Data moves between devices by JAX's collectives and lax.ppermute only.
A program may use at most 64 MiB of HBM per device.

v0:
```python
import math
import jax
import jax.numpy as jnp
from jax import lax
from jax.sharding import PartitionSpec as P

N = 6144


def partner(value, axis, apart):
    mask = 2**apart
    pairs = [(source, source ^ mask) for source in range(lax.axis_size(axis))]
    return lax.ppermute(value, axis, pairs)


def local(pressure):
    block_rows = pressure.shape[1]
    block_cols = pressure.shape[2]
    shot_index = lax.axis_index("shot")
    recv_index = lax.axis_index("recv")
    grid_row = recv_index // 2
    pair_bit = recv_index % 2
    mirror = pressure
    levels = lax.axis_size("shot").bit_length() - 1
    for bit_index in range(levels):
        stride = 2**bit_index
        agrees = shot_index // stride % 2 == grid_row // stride % 2
        transit = partner(mirror, "shot", bit_index)
        arrived = partner(transit, "recv", bit_index + 1)
        mirror = jnp.where(agrees, mirror, arrived)
    kept_cols = lax.dynamic_slice_in_dim(mirror, pair_bit * block_rows, block_rows, 2)
    given_cols = lax.dynamic_slice_in_dim(mirror, (1 - pair_bit) * block_rows, block_rows, 2)
    taken_cols = partner(given_cols, "recv", 0)
    stacked = jnp.where(
        pair_bit == 0,
        jnp.concatenate([kept_cols, taken_cols], axis=1),
        jnp.concatenate([taken_cols, kept_cols], axis=1),
    )
    symmetric = (
        (pressure.astype(jnp.float32) + jnp.swapaxes(stacked, 1, 2).astype(jnp.float32)) * 0.5
    ).astype(jnp.bfloat16)
    factor = 1.0 / math.sqrt(N)
    row_panel = lax.all_gather(symmetric, "shot", axis=2, tiled=True)
    shard_block = lax.all_gather(symmetric, "recv", axis=1, tiled=True)
    left_real = row_panel[0]
    left_imag = row_panel[1]
    upper_half = jnp.concatenate([shard_block[0], shard_block[1]], axis=1)
    lower_half = jnp.concatenate([-shard_block[1], shard_block[0]], axis=1)
    running = jnp.dot(left_real, upper_half, preferred_element_type=jnp.float32)
    running = running + jnp.dot(left_imag, lower_half, preferred_element_type=jnp.float32)
    running = running * factor
    return jnp.stack([running[:, :block_cols], running[:, block_cols:]])


def solution(mesh):
    placed = (P(None, "recv", "shot"),)
    return jax.shard_map(
        local, mesh=mesh, in_specs=placed, out_specs=P(None, "recv", "shot"), check_vma=False
    )
```

profile of v0, /device:TPU:2, one launch (start us, length us, event | category | flops | bytes accessed | tf_op | source)
XLA Modules:
  0.0 570.4 jit_solution(5705940932931412052)
XLA Ops:
  6.5 0.0 copy-start.3
  6.5 0.0 all-gather.5.cloned.1.call-start
  6.5 1.2 copy.3
  7.7 1.9 collective-permute-start
  9.7 1.7 collective-permute-done
  11.4 4.0 collective-permute-start.1
  15.4 10.5 %collective-permute-done.1 = bf16[2,192,384]{1,2,0:T(8,128)(2,1)S(1)} collective-permute-done((bf16[2,192,384]{1,2,0:T(8,128)(2,1)S(1)}, bf16[2,192,384]{1,2,0:T(8,128)(2,1)S(1)}, u32[]{:S(2)}, u32[]{:S(2)}) %collective-permute-start.1) | collective-permute-done | bytes 294944 | tf_op jit(solution)/shard_map/ppermute | solution.py:13
  25.9 3.8 collective-permute-start.2
  29.8 8.6 %collective-permute-done.2 = bf16[2,192,384]{1,2,0:T(8,128)(2,1)S(1)} collective-permute-done((bf16[2,192,384]{1,2,0:T(8,128)(2,1)S(1)}, bf16[2,192,384]{1,2,0:T(8,128)(2,1)S(1)}, u32[]{:S(2)}, u32[]{:S(2)}) %collective-permute-start.2) | collective-permute-done | bytes 294944 | tf_op jit(solution)/shard_map/ppermute | solution.py:13
  38.4 3.5 collective-permute-start.3
  41.9 7.9 %collective-permute-done.3 = bf16[2,192,384]{1,2,0:T(8,128)(2,1)S(1)} collective-permute-done((bf16[2,192,384]{1,2,0:T(8,128)(2,1)S(1)}, bf16[2,192,384]{1,2,0:T(8,128)(2,1)S(1)}, u32[]{:S(2)}, u32[]{:S(2)}) %collective-permute-start.3) | collective-permute-done | bytes 294944 | tf_op jit(solution)/shard_map/ppermute | solution.py:13
  49.9 5.2 collective-permute-start.4
  55.1 15.3 %collective-permute-done.4 = bf16[2,192,384]{1,2,0:T(8,128)(2,1)S(1)} collective-permute-done((bf16[2,192,384]{1,2,0:T(8,128)(2,1)S(1)}, bf16[2,192,384]{1,2,0:T(8,128)(2,1)S(1)}, u32[]{:S(2)}, u32[]{:S(2)}) %collective-permute-start.4) | collective-permute-done | bytes 294944 | tf_op jit(solution)/shard_map/ppermute | solution.py:13
  70.4 5.1 collective-permute-start.5
  75.6 8.4 %collective-permute-done.5 = bf16[2,192,384]{1,2,0:T(8,128)(2,1)S(1)} collective-permute-done((bf16[2,192,384]{1,2,0:T(8,128)(2,1)S(1)}, bf16[2,192,384]{1,2,0:T(8,128)(2,1)S(1)}, u32[]{:S(2)}, u32[]{:S(2)}) %collective-permute-start.5) | collective-permute-done | bytes 294944 | tf_op jit(solution)/shard_map/ppermute | solution.py:13
  84.0 9.1 %collective-permute-start.6 = (bf16[2,192,384]{1,2,0:T(8,128)(2,1)S(1)}, bf16[2,192,384]{1,2,0:T(8,128)(2,1)S(1)}, u32[]{:S(2)}, u32[]{:S(2)}) collective-permute-start(bf16[2,192,384]{1,2,0:T(8,128)(2,1)S(1)} %broadcast_select_fusion.2), channel_id=1, source_target_pairs={{0,256},{32,288},{64,320},{96,352},{128,384},{160,416},{192,448},{... | collective-permute-start | bytes 884744 | tf_op jit(solution)/shard_map/ppermute | solution.py:13
  93.1 31.7 %collective-permute-done.6 = bf16[2,192,384]{1,2,0:T(8,128)(2,1)S(1)} collective-permute-done((bf16[2,192,384]{1,2,0:T(8,128)(2,1)S(1)}, bf16[2,192,384]{1,2,0:T(8,128)(2,1)S(1)}, u32[]{:S(2)}, u32[]{:S(2)}) %collective-permute-start.6) | collective-permute-done | bytes 294944 | tf_op jit(solution)/shard_map/ppermute | solution.py:13
  124.8 21.9 %collective-permute-start.7 = (bf16[2,192,384]{1,2,0:T(8,128)(2,1)S(1)}, bf16[2,192,384]{1,2,0:T(8,128)(2,1)S(1)}, u32[]{:S(2)}, u32[]{:S(2)}) collective-permute-start(bf16[2,192,384]{1,2,0:T(8,128)(2,1)S(1)} %collective-permute-done.6), channel_id=1, source_target_pairs={{0,16},{1,17},{2,18},{3,19},{4,20},{5,21},{6,22},{7,23},{8,24},{9,... | collective-permute-start | bytes 884744 | tf_op jit(solution)/shard_map/ppermute | solution.py:13
  146.8 14.6 %collective-permute-done.7 = bf16[2,192,384]{1,2,0:T(8,128)(2,1)S(1)} collective-permute-done((bf16[2,192,384]{1,2,0:T(8,128)(2,1)S(1)}, bf16[2,192,384]{1,2,0:T(8,128)(2,1)S(1)}, u32[]{:S(2)}, u32[]{:S(2)}) %collective-permute-start.7) | collective-permute-done | bytes 294944 | tf_op jit(solution)/shard_map/ppermute | solution.py:13
  161.4 2.4 collective-permute-start.8
  163.9 6.2 %collective-permute-done.8 = bf16[2,192,192]{1,2,0:T(8,128)(2,1)S(1)} collective-permute-done((bf16[2,192,192]{1,2,0:T(8,128)(2,1)S(1)}, bf16[2,192,192]{1,2,0:T(8,128)(2,1)S(1)}, u32[]{:S(2)}, u32[]{:S(2)}) %collective-permute-start.8) | collective-permute-done | bytes 147488 | tf_op jit(solution)/shard_map/ppermute | solution.py:13
  170.1 0.0 copy-done.3
  170.1 1.0 fusion.15
  171.1 0.0 all-gather.5.cloned.1.call-update
  171.1 0.0 all-gather.3.cloned.1.call-start
  171.2 0.7 all-gather.3.cloned.1.call-update
  171.9 269.1 %all-gather.5.cloned.1.call-done = bf16[2,6144,384]{2,1,0:T(8,128)(2,1)} async-done(((bf16[2,192,384]{2,1,0:T(8,128)(2,1)}), bf16[2,6144,384]{2,1,0:T(8,128)(2,1)}) %all-gather.5.cloned.1.call-update) | async-done | bytes 9437200 | tf_op jit(solution)/shard_map/all_gather | solution.py:44
  440.9 0.0 copy-start
  440.9 5.3 fusion.18
  446.2 1.5 copy-done
  447.7 4.6 slice_bitcast_fusion.1
  452.4 99.8 %all-gather.3.cloned.1.call-done = bf16[2,192,6144]{2,1,0:T(8,128)(2,1)} async-done(((bf16[2,192,384]{2,1,0:T(8,128)(2,1)}), bf16[2,192,6144]{2,1,0:T(8,128)(2,1)}) %all-gather.3.cloned.1.call-update) | async-done | bytes 4718608 | tf_op jit(solution)/shard_map/all_gather | solution.py:43
  552.1 0.0 copy-start.1
  552.1 0.0 copy-start.2
  552.1 0.0 copy-start.4
  552.1 6.5 %fusion = f32[192,768]{1,0:T(8,128)S(1)} fusion(bf16[6144,384]{1,0:T(8,128)(2,1)} %get-tuple-element.6, bf16[6144,384]{1,0:T(8,128)(2,1)} %get-tuple-element.5, bf16[2,192,6144]{2,1,0:T(8,128)(2,1)} %all-gather.3.cloned.1.call-done), kind=kOutput, calls=%fused_computation | convolution fusion | flops 1830813696 | bytes 12386304 | tf_op jit(solution)/shard_map/dot_general | solution.py:49
  558.7 0.0 copy-done.1
  558.7 0.6 copy-done.2
  559.3 1.3 copy-done.4
  560.7 2.0 fusion.11
  562.7 0.9 pad_maximum_fusion
  (6 shorter events, 0.2 us)
Async XLA Ops:
  6.5 163.6 %copy-start.3 = (bf16[2,192,384]{2,1,0:T(8,128)(2,1)S(1)}, bf16[2,192,384]{2,1,0:T(8,128)(2,1)}, u32[]{:S(2)}) copy-start(bf16[2,192,384]{2,1,0:T(8,128)(2,1)} %param.1) | copy-start | bytes 884740
  6.5 434.4 %all-gather.5.cloned.1.call-start = ((), (), s32[]{:S(2)}) async-start(), calls=%async_computation.1 | async-start | bytes 9732096 | tf_op jit(solution)/shard_map/all_gather | solution.py:44
  7.7 3.6 collective-permute-start
  11.4 14.5 %collective-permute-start.1 = (bf16[2,192,384]{1,2,0:T(8,128)(2,1)S(1)}, bf16[2,192,384]{1,2,0:T(8,128)(2,1)S(1)}, u32[]{:S(2)}, u32[]{:S(2)}) collective-permute-start(bf16[2,192,384]{1,2,0:T(8,128)(2,1)S(1)} %collective-permute-done), channel_id=1, source_target_pairs={{0,2},{1,3},{2,0},{3,1},{4,6},{5,7},{6,4},{7,5},{8,10},{9,11},{10,... | collective-permute-start | bytes 884744 | tf_op jit(solution)/shard_map/ppermute | solution.py:13
  25.9 12.4 %collective-permute-start.2 = (bf16[2,192,384]{1,2,0:T(8,128)(2,1)S(1)}, bf16[2,192,384]{1,2,0:T(8,128)(2,1)S(1)}, u32[]{:S(2)}, u32[]{:S(2)}) collective-permute-start(bf16[2,192,384]{1,2,0:T(8,128)(2,1)S(1)} %broadcast_select_fusion), channel_id=1, source_target_pairs={{0,64},{32,96},{64,0},{96,32},{128,192},{160,224},{192,128},{224,1... | collective-permute-start | bytes 884744 | tf_op jit(solution)/shard_map/ppermute | solution.py:13
  38.4 11.5 %collective-permute-start.3 = (bf16[2,192,384]{1,2,0:T(8,128)(2,1)S(1)}, bf16[2,192,384]{1,2,0:T(8,128)(2,1)S(1)}, u32[]{:S(2)}, u32[]{:S(2)}) collective-permute-start(bf16[2,192,384]{1,2,0:T(8,128)(2,1)S(1)} %collective-permute-done.2), channel_id=1, source_target_pairs={{0,4},{1,5},{2,6},{3,7},{4,0},{5,1},{6,2},{7,3},{8,12},{9,13},{10,... | collective-permute-start | bytes 884744 | tf_op jit(solution)/shard_map/ppermute | solution.py:13
  49.9 20.5 %collective-permute-start.4 = (bf16[2,192,384]{1,2,0:T(8,128)(2,1)S(1)}, bf16[2,192,384]{1,2,0:T(8,128)(2,1)S(1)}, u32[]{:S(2)}, u32[]{:S(2)}) collective-permute-start(bf16[2,192,384]{1,2,0:T(8,128)(2,1)S(1)} %broadcast_select_fusion.1), channel_id=1, source_target_pairs={{0,128},{32,160},{64,192},{96,224},{128,0},{160,32},{192,64},{224,... | collective-permute-start | bytes 884744 | tf_op jit(solution)/shard_map/ppermute | solution.py:13
  70.4 13.5 %collective-permute-start.5 = (bf16[2,192,384]{1,2,0:T(8,128)(2,1)S(1)}, bf16[2,192,384]{1,2,0:T(8,128)(2,1)S(1)}, u32[]{:S(2)}, u32[]{:S(2)}) collective-permute-start(bf16[2,192,384]{1,2,0:T(8,128)(2,1)S(1)} %collective-permute-done.4), channel_id=1, source_target_pairs={{0,8},{1,9},{2,10},{3,11},{4,12},{5,13},{6,14},{7,15},{8,0},{9,1},... | collective-permute-start | bytes 884744 | tf_op jit(solution)/shard_map/ppermute | solution.py:13
  84.0 40.8 %collective-permute-start.6 = (bf16[2,192,384]{1,2,0:T(8,128)(2,1)S(1)}, bf16[2,192,384]{1,2,0:T(8,128)(2,1)S(1)}, u32[]{:S(2)}, u32[]{:S(2)}) collective-permute-start(bf16[2,192,384]{1,2,0:T(8,128)(2,1)S(1)} %broadcast_select_fusion.2), channel_id=1, source_target_pairs={{0,256},{32,288},{64,320},{96,352},{128,384},{160,416},{192,448},{... | collective-permute-start | bytes 884744 | tf_op jit(solution)/shard_map/ppermute | solution.py:13
  124.8 36.5 %collective-permute-start.7 = (bf16[2,192,384]{1,2,0:T(8,128)(2,1)S(1)}, bf16[2,192,384]{1,2,0:T(8,128)(2,1)S(1)}, u32[]{:S(2)}, u32[]{:S(2)}) collective-permute-start(bf16[2,192,384]{1,2,0:T(8,128)(2,1)S(1)} %collective-permute-done.6), channel_id=1, source_target_pairs={{0,16},{1,17},{2,18},{3,19},{4,20},{5,21},{6,22},{7,23},{8,24},{9,... | collective-permute-start | bytes 884744 | tf_op jit(solution)/shard_map/ppermute | solution.py:13
  161.4 8.6 %collective-permute-start.8 = (bf16[2,192,192]{1,2,0:T(8,128)(2,1)S(1)}, bf16[2,192,192]{1,2,0:T(8,128)(2,1)S(1)}, u32[]{:S(2)}, u32[]{:S(2)}) collective-permute-start(bf16[2,192,192]{1,2,0:T(8,128)(2,1)S(1)} %get-tuple-element.10), channel_id=1, source_target_pairs={{0,1},{1,0},{2,3},{3,2},{4,5},{5,4},{6,7},{7,6},{8,9},{9,8},{10,11... | collective-permute-start | bytes 442376 | tf_op jit(solution)/shard_map/ppermute | solution.py:13
  171.1 381.0 %all-gather.3.cloned.1.call-start = ((), (), s32[]{:S(2)}) async-start(), calls=%async_computation | async-start | bytes 5013504 | tf_op jit(solution)/shard_map/all_gather | solution.py:43
  440.9 6.8 %copy-start = (bf16[2,6144,384]{2,1,0:T(8,128)(2,1)S(1)}, bf16[2,6144,384]{2,1,0:T(8,128)(2,1)}, u32[]{:S(2)}) copy-start(bf16[2,6144,384]{2,1,0:T(8,128)(2,1)} %all-gather.5.cloned.1.call-done) | copy-start | bytes 28311556
  552.1 6.5 %copy-start.1 = (bf16[6144,384]{1,0:T(8,128)(2,1)S(1)}, bf16[6144,384]{1,0:T(8,128)(2,1)}, u32[]{:S(2)}) copy-start(bf16[6144,384]{1,0:T(8,128)(2,1)} %fusion.18) | copy-start | bytes 14155780
  552.1 7.2 %copy-start.2 = (bf16[6144,384]{1,0:T(8,128)(2,1)S(1)}, bf16[6144,384]{1,0:T(8,128)(2,1)}, u32[]{:S(2)}) copy-start(bf16[6144,384]{1,0:T(8,128)(2,1)} %get-tuple-element.5) | copy-start | bytes 14155780
  552.1 8.5 %copy-start.4 = (bf16[2,192,6144]{2,1,0:T(8,128)(2,1)S(1)}, bf16[2,192,6144]{2,1,0:T(8,128)(2,1)}, u32[]{:S(2)}) copy-start(bf16[2,192,6144]{2,1,0:T(8,128)(2,1)} %all-gather.3.cloned.1.call-done) | copy-start | bytes 14155780
Sparse Core Ops, SparseCore 0:
  171.2 269.6 all-gather.4
  443.0 109.0 all-gather.2
where the time goes:
time: 571 us; the launch traced here: 570 us
  waiting for transfers between devices  474 us (83%)
  starting transfers between devices  57 us (10%)
  between operations  13.8 us (2%)
  local copies, waits for them, and re-layouts  9.36 us (2%)
  matrix products  8.52 us (1%)
  other arithmetic  7.32 us (1%)
    all_gather x1, waiting for transfers between devices, local(): shard_block = lax.all_gather(symmetric, 'recv', axis=1, tiled=True)  269 us
    ppermute x9, waiting for transfers between devices, partner(): return lax.ppermute(value, axis, pairs)  105 us
    all_gather x1, waiting for transfers between devices, local(): row_panel = lax.all_gather(symmetric, 'shot', axis=2, tiled=True)  99.8 us
    ppermute x9, starting transfers between devices, partner(): return lax.ppermute(value, axis, pairs)  56.9 us
  transfers between devices with their start and end apart: 11, of which 11 were waited for; matrix products, arithmetic and copies ran while one was open for 2% of the time, Pallas kernels for 0%

commit v1 on v0

--- a/solution.py
+++ b/solution.py
@@ -41,7 +41,10 @@
     ).astype(jnp.bfloat16)
     factor = 1.0 / math.sqrt(N)
     row_panel = lax.all_gather(symmetric, "shot", axis=2, tiled=True)
-    shard_block = lax.all_gather(symmetric, "recv", axis=1, tiled=True)
+    devices = lax.axis_size("recv")
+    shards = jnp.stack([symmetric for _ in range(devices)])
+    shards = lax.all_to_all(shards, "recv", split_axis=0, concat_axis=0)
+    shard_block = jnp.concatenate(shards, axis=1)
     left_real = row_panel[0]
     left_imag = row_panel[1]
     upper_half = jnp.concatenate([shard_block[0], shard_block[1]], axis=1)

time: 571 us -> 709 us (1.24)
  the two profiles are of different devices: /device:TPU:2 before, /device:TPU:469 now
where the time goes in v1:
time: 709 us
  waiting for transfers between devices  623 us (88%)
  starting transfers between devices  41.8 us (6%)
  local copies, waits for them, and re-layouts  17.3 us (2%)
  between operations  13.8 us (2%)
  matrix products  8.52 us (1%)
    all_to_all x1, waiting for transfers between devices, local(): shards = lax.all_to_all(shards, 'recv', split_axis=0, concat_axis=0)  506 us
    ppermute x9, waiting for transfers between devices, partner(): return lax.ppermute(value, axis, pairs)  116 us
    ppermute x9, starting transfers between devices, partner(): return lax.ppermute(value, axis, pairs)  25.2 us
    all_to_all x1, starting transfers between devices, local(): shards = lax.all_to_all(shards, 'recv', split_axis=0, concat_axis=0)  16.5 us
  transfers between devices with their start and end apart: 11, of which 10 were waited for; matrix products, arithmetic and copies ran while one was open for 1% of the time, Pallas kernels for 0%

profile of v1, /device:TPU:469, one launch (start us, length us, event | category | flops | bytes accessed | tf_op | source)
XLA Modules:
  0.0 708.5 jit_solution(13855503193652914772)
XLA Ops:
  6.5 0.0 copy-start.3
  6.5 1.2 copy.3
  7.7 2.6 collective-permute-start
  10.3 1.3 collective-permute-done
  11.7 2.1 collective-permute-start.1
  13.8 11.5 %collective-permute-done.1 = bf16[2,192,384]{1,2,0:T(8,128)(2,1)S(1)} collective-permute-done((bf16[2,192,384]{1,2,0:T(8,128)(2,1)S(1)}, bf16[2,192,384]{1,2,0:T(8,128)(2,1)S(1)}, u32[]{:S(2)}, u32[]{:S(2)}) %collective-permute-start.1) | collective-permute-done | bytes 294944 | tf_op jit(solution)/shard_map/ppermute | solution.py:13
  25.4 2.6 collective-permute-start.2
  28.1 8.6 %collective-permute-done.2 = bf16[2,192,384]{1,2,0:T(8,128)(2,1)S(1)} collective-permute-done((bf16[2,192,384]{1,2,0:T(8,128)(2,1)S(1)}, bf16[2,192,384]{1,2,0:T(8,128)(2,1)S(1)}, u32[]{:S(2)}, u32[]{:S(2)}) %collective-permute-start.2) | collective-permute-done | bytes 294944 | tf_op jit(solution)/shard_map/ppermute | solution.py:13
  36.7 2.9 collective-permute-start.3
  39.7 7.4 %collective-permute-done.3 = bf16[2,192,384]{1,2,0:T(8,128)(2,1)S(1)} collective-permute-done((bf16[2,192,384]{1,2,0:T(8,128)(2,1)S(1)}, bf16[2,192,384]{1,2,0:T(8,128)(2,1)S(1)}, u32[]{:S(2)}, u32[]{:S(2)}) %collective-permute-start.3) | collective-permute-done | bytes 294944 | tf_op jit(solution)/shard_map/ppermute | solution.py:13
  47.1 3.1 collective-permute-start.4
  50.2 16.7 %collective-permute-done.4 = bf16[2,192,384]{1,2,0:T(8,128)(2,1)S(1)} collective-permute-done((bf16[2,192,384]{1,2,0:T(8,128)(2,1)S(1)}, bf16[2,192,384]{1,2,0:T(8,128)(2,1)S(1)}, u32[]{:S(2)}, u32[]{:S(2)}) %collective-permute-start.4) | collective-permute-done | bytes 294944 | tf_op jit(solution)/shard_map/ppermute | solution.py:13
  66.9 2.0 collective-permute-start.5
  69.0 11.0 %collective-permute-done.5 = bf16[2,192,384]{1,2,0:T(8,128)(2,1)S(1)} collective-permute-done((bf16[2,192,384]{1,2,0:T(8,128)(2,1)S(1)}, bf16[2,192,384]{1,2,0:T(8,128)(2,1)S(1)}, u32[]{:S(2)}, u32[]{:S(2)}) %collective-permute-start.5) | collective-permute-done | bytes 294944 | tf_op jit(solution)/shard_map/ppermute | solution.py:13
  80.0 5.2 collective-permute-start.6
  85.2 28.0 %collective-permute-done.6 = bf16[2,192,384]{1,2,0:T(8,128)(2,1)S(1)} collective-permute-done((bf16[2,192,384]{1,2,0:T(8,128)(2,1)S(1)}, bf16[2,192,384]{1,2,0:T(8,128)(2,1)S(1)}, u32[]{:S(2)}, u32[]{:S(2)}) %collective-permute-start.6) | collective-permute-done | bytes 294944 | tf_op jit(solution)/shard_map/ppermute | solution.py:13
  113.1 1.9 collective-permute-start.7
  115.2 27.1 %collective-permute-done.7 = bf16[2,192,384]{1,2,0:T(8,128)(2,1)S(1)} collective-permute-done((bf16[2,192,384]{1,2,0:T(8,128)(2,1)S(1)}, bf16[2,192,384]{1,2,0:T(8,128)(2,1)S(1)}, u32[]{:S(2)}, u32[]{:S(2)}) %collective-permute-start.7) | collective-permute-done | bytes 294944 | tf_op jit(solution)/shard_map/ppermute | solution.py:13
  142.3 2.8 collective-permute-start.8
  145.1 4.7 collective-permute-done.8
  149.9 0.0 copy-done.3
  149.9 0.3 fusion.15
  150.2 0.0 copy-start.2
  150.2 5.2 stack.8
  155.3 0.0 copy-done.2
  155.3 16.5 %all-to-all-start = ((bf16[32,2,192,384]{3,2,1,0:T(8,128)(2,1)}), bf16[32,2,192,384]{3,2,1,0:T(8,128)(2,1)}, u32[]{:S(2)}, u32[]{:S(2)}) async-start(bf16[32,2,192,384]{3,2,1,0:T(8,128)(2,1)} %stack.8), calls=%async_computation | async-start | bytes 18874368 | tf_op jit(solution)/shard_map/all_to_all | solution.py:46
  171.9 0.0 all-gather.2.cloned.1.call-start
  171.9 0.7 all-gather.2.cloned.1.call-update
  172.6 505.7 %all-to-all-done = bf16[32,2,192,384]{3,2,1,0:T(8,128)(2,1)} async-done(((bf16[32,2,192,384]{3,2,1,0:T(8,128)(2,1)}), bf16[32,2,192,384]{3,2,1,0:T(8,128)(2,1)}, u32[]{:S(2)}, u32[]{:S(2)}) %all-to-all-start) | async-done | bytes 9437216 | tf_op jit(solution)/shard_map/all_to_all | solution.py:46
  678.3 7.0 fusion.18
  685.2 0.0 copy-start
  685.3 2.1 copy-done
  687.4 0.0 slice-start
  687.4 3.0 bitcast_negate_fusion
  690.4 0.0 all-gather.2.cloned.1.call-done
  690.4 0.0 copy-start.1
  690.4 0.0 slice-start.1
  690.4 0.0 copy-start.4
  690.4 6.5 fusion
  697.0 0.0 slice-done
  697.0 0.0 copy-done.1
  697.0 0.5 slice-done.1
  697.4 1.3 copy-done.4
  698.8 2.0 fusion.11
  700.8 0.9 pad_maximum_fusion
  (7 shorter events, 0.2 us)
Async XLA Ops:
  6.5 143.3 %copy-start.3 = (bf16[2,192,384]{2,1,0:T(8,128)(2,1)S(1)}, bf16[2,192,384]{2,1,0:T(8,128)(2,1)}, u32[]{:S(2)}) copy-start(bf16[2,192,384]{2,1,0:T(8,128)(2,1)} %param.1) | copy-start | bytes 884740
  7.7 3.9 collective-permute-start
  11.7 13.7 %collective-permute-start.1 = (bf16[2,192,384]{1,2,0:T(8,128)(2,1)S(1)}, bf16[2,192,384]{1,2,0:T(8,128)(2,1)S(1)}, u32[]{:S(2)}, u32[]{:S(2)}) collective-permute-start(bf16[2,192,384]{1,2,0:T(8,128)(2,1)S(1)} %collective-permute-done), channel_id=1, source_target_pairs={{0,2},{1,3},{2,0},{3,1},{4,6},{5,7},{6,4},{7,5},{8,10},{9,11},{10,... | collective-permute-start | bytes 884744 | tf_op jit(solution)/shard_map/ppermute | solution.py:13
  25.4 11.3 %collective-permute-start.2 = (bf16[2,192,384]{1,2,0:T(8,128)(2,1)S(1)}, bf16[2,192,384]{1,2,0:T(8,128)(2,1)S(1)}, u32[]{:S(2)}, u32[]{:S(2)}) collective-permute-start(bf16[2,192,384]{1,2,0:T(8,128)(2,1)S(1)} %broadcast_select_fusion), channel_id=1, source_target_pairs={{0,64},{32,96},{64,0},{96,32},{128,192},{160,224},{192,128},{224,1... | collective-permute-start | bytes 884744 | tf_op jit(solution)/shard_map/ppermute | solution.py:13
  36.7 10.4 %collective-permute-start.3 = (bf16[2,192,384]{1,2,0:T(8,128)(2,1)S(1)}, bf16[2,192,384]{1,2,0:T(8,128)(2,1)S(1)}, u32[]{:S(2)}, u32[]{:S(2)}) collective-permute-start(bf16[2,192,384]{1,2,0:T(8,128)(2,1)S(1)} %collective-permute-done.2), channel_id=1, source_target_pairs={{0,4},{1,5},{2,6},{3,7},{4,0},{5,1},{6,2},{7,3},{8,12},{9,13},{10,... | collective-permute-start | bytes 884744 | tf_op jit(solution)/shard_map/ppermute | solution.py:13
  47.1 19.8 %collective-permute-start.4 = (bf16[2,192,384]{1,2,0:T(8,128)(2,1)S(1)}, bf16[2,192,384]{1,2,0:T(8,128)(2,1)S(1)}, u32[]{:S(2)}, u32[]{:S(2)}) collective-permute-start(bf16[2,192,384]{1,2,0:T(8,128)(2,1)S(1)} %broadcast_select_fusion.1), channel_id=1, source_target_pairs={{0,128},{32,160},{64,192},{96,224},{128,0},{160,32},{192,64},{224,... | collective-permute-start | bytes 884744 | tf_op jit(solution)/shard_map/ppermute | solution.py:13
  66.9 13.0 %collective-permute-start.5 = (bf16[2,192,384]{1,2,0:T(8,128)(2,1)S(1)}, bf16[2,192,384]{1,2,0:T(8,128)(2,1)S(1)}, u32[]{:S(2)}, u32[]{:S(2)}) collective-permute-start(bf16[2,192,384]{1,2,0:T(8,128)(2,1)S(1)} %collective-permute-done.4), channel_id=1, source_target_pairs={{0,8},{1,9},{2,10},{3,11},{4,12},{5,13},{6,14},{7,15},{8,0},{9,1},... | collective-permute-start | bytes 884744 | tf_op jit(solution)/shard_map/ppermute | solution.py:13
  80.0 33.2 %collective-permute-start.6 = (bf16[2,192,384]{1,2,0:T(8,128)(2,1)S(1)}, bf16[2,192,384]{1,2,0:T(8,128)(2,1)S(1)}, u32[]{:S(2)}, u32[]{:S(2)}) collective-permute-start(bf16[2,192,384]{1,2,0:T(8,128)(2,1)S(1)} %broadcast_select_fusion.2), channel_id=1, source_target_pairs={{0,256},{32,288},{64,320},{96,352},{128,384},{160,416},{192,448},{... | collective-permute-start | bytes 884744 | tf_op jit(solution)/shard_map/ppermute | solution.py:13
  113.1 29.1 %collective-permute-start.7 = (bf16[2,192,384]{1,2,0:T(8,128)(2,1)S(1)}, bf16[2,192,384]{1,2,0:T(8,128)(2,1)S(1)}, u32[]{:S(2)}, u32[]{:S(2)}) collective-permute-start(bf16[2,192,384]{1,2,0:T(8,128)(2,1)S(1)} %collective-permute-done.6), channel_id=1, source_target_pairs={{0,16},{1,17},{2,18},{3,19},{4,20},{5,21},{6,22},{7,23},{8,24},{9,... | collective-permute-start | bytes 884744 | tf_op jit(solution)/shard_map/ppermute | solution.py:13
  142.3 7.6 %collective-permute-start.8 = (bf16[2,192,192]{1,2,0:T(8,128)(2,1)S(1)}, bf16[2,192,192]{1,2,0:T(8,128)(2,1)S(1)}, u32[]{:S(2)}, u32[]{:S(2)}) collective-permute-start(bf16[2,192,192]{1,2,0:T(8,128)(2,1)S(1)} %get-tuple-element.10), channel_id=1, source_target_pairs={{0,1},{1,0},{2,3},{3,2},{4,5},{5,4},{6,7},{7,6},{8,9},{9,8},{10,11... | collective-permute-start | bytes 442376 | tf_op jit(solution)/shard_map/ppermute | solution.py:13
  150.2 5.2 copy-start.2
  155.3 523.0 %all-to-all-start = ((bf16[32,2,192,384]{3,2,1,0:T(8,128)(2,1)}), bf16[32,2,192,384]{3,2,1,0:T(8,128)(2,1)}, u32[]{:S(2)}, u32[]{:S(2)}) async-start(bf16[32,2,192,384]{3,2,1,0:T(8,128)(2,1)} %stack.8), calls=%async_computation | async-start | bytes 18874368 | tf_op jit(solution)/shard_map/all_to_all | solution.py:46
  171.9 518.5 %all-gather.2.cloned.1.call-start = ((), (), s32[]{:S(2)}) async-start(), calls=%async_computation.1 | async-start | bytes 5013504 | tf_op jit(solution)/shard_map/all_gather | solution.py:43
  685.2 2.1 copy-start
  687.4 9.6 %slice-start = ((s8[4718592]{0:T(1024)(128)(4,1)}), s8[524288]{0:T(1024)(128)(4,1)S(1)}, s32[]{:S(2)}) async-start(s8[4718592]{0:T(1024)(128)(4,1)} %bitcast.26), calls=%async_computation.2 | async-start | bytes 1048576
  690.4 6.6 copy-start.1
  690.4 7.0 slice-start.1
  690.4 8.4 %copy-start.4 = (bf16[2,192,6144]{2,1,0:T(8,128)(2,1)S(1)}, bf16[2,192,6144]{2,1,0:T(8,128)(2,1)}, u32[]{:S(2)}) copy-start(bf16[2,192,6144]{2,1,0:T(8,128)(2,1)} %all-gather.2.cloned.1.call-done) | copy-start | bytes 14155780
Sparse Core Ops, SparseCore 0:
  174.8 406.7 all-gather.1
